TPU v7x, 32 devices: a whole 2x2x4 slice. The times are simulated.
32 devices in a mesh: groups: 2 (over x), src: 8 (over z, y), tile: 2 (over core).
Axes of the slice: x: 2, y: 2, z: 4, core: 2. Of those that a mesh axis runs over, the one named last changes fastest.
Arguments:
- mask: float32 [2048, 1024], P(('groups', 'tile')), parts along dimension 0, may hold values from 0 to 1
- target: float32 [2048, 1024], P(('groups', 'tile')), parts along dimension 0, may hold values from 0 to 1
- pupil: float32 [64, 64], replicated, may hold values from 0.1 to 1.9
- source_shift: int32 [24, 2], replicated, may hold values from -24 to 24
- source_weight: float32 [24], replicated, may hold values from 0.25 to 4
Outputs:
- mask_gradient: float32 [2048, 1024], P(('groups', 'tile'), 'src'), parts along dimension 0
There are 2 independent parts, one for each index of `groups`. A program takes and returns all parts, laid end to end along the dimension named above; an argument that names none is the same for every part. Nothing has to cross between parts.
Inputs may be any that keep to these rules, and one draw needn't show every extreme that they name: `source_shift`: integer frequency shifts of the source points.
All inputs are finite; a program needn't handle non-finite values.
Results may differ from a plain program's by a relative error of at most 0.0003.
Values sent between devices are 32-bit elements; how exact they have to be, the bound alone decides.
A program may use at most 128 MiB of HBM per device.

v0:
```python
import numpy as np

import jax
import jax.numpy as jnp
from jax import lax
from jax.sharding import PartitionSpec as P

TS = 512
HALO = 64
PAD = 640
GRID = 128
REACH = 24

exact_mode = lax.Precision.HIGHEST
resist_gain = 25.0
resist_level = 0.25


def tables(freqs, columns):
    pixels = np.arange(PAD)[:, None]
    samples = np.arange(GRID)[None, :] * (PAD // GRID)
    spread = np.ones((PAD, GRID))
    for p in range(1, GRID // 2):
        spread += 2.0 * np.cos(2.0 * np.pi * (p * (pixels - samples) % PAD) / PAD)
    spread /= GRID
    tiles = columns // TS
    across = np.zeros((columns, tiles * GRID))
    for c in range(tiles):
        low, high = max(0, c * TS - HALO), min(columns, c * TS - HALO + PAD)
        across[low:high, c * GRID : (c + 1) * GRID] = spread[low + HALO - c * TS : high + HALO - c * TS]
    bins = np.arange(-freqs // 2 - REACH, freqs // 2 + REACH)[:, None] * np.arange(GRID)[None, :]
    angle = 2.0 * np.pi * (bins % GRID) / GRID
    waves = np.concatenate([np.cos(angle), np.sin(angle)], axis=1)
    return spread, across, waves


def rotation(waves, freqs):
    centre = waves[REACH : REACH + freqs]
    cosine, sine = centre[:, :GRID].T, centre[:, GRID:].T
    return np.block([[cosine, -sine], [sine, cosine]])


def mm(a, b):
    return jnp.dot(a, b, precision=exact_mode, preferred_element_type=jnp.float32)


def resist_slope(intensity, target):
    printed = jax.nn.sigmoid(resist_gain * (intensity - resist_level))
    return 2.0 * (printed - target) * resist_gain * printed * (1.0 - printed)


def halves(y, tiles, freqs):
    real, imag = [], []
    for c in range(tiles):
        top = y[2 * c * freqs : (2 * c + 1) * freqs]
        low = y[(2 * c + 1) * freqs : (2 * c + 2) * freqs]
        real.append(top[:, :GRID] - low[:, GRID:])
        imag.append(top[:, GRID:] + low[:, :GRID])
    return jnp.concatenate(real, axis=1), jnp.concatenate(imag, axis=1)


def shards(mask, target, pupil, source_shift, source_weight):
    f32 = jnp.float32
    me = lax.axis_index("src")
    n = lax.axis_size("src")
    nt = lax.axis_size("tile")
    own = source_shift.shape[0] // n
    freqs = pupil.shape[0]
    columns = mask.shape[1]
    tiles = columns // TS
    width = columns // n
    spread64, across64, waves64 = tables(freqs, columns)
    spread = jnp.asarray(spread64, f32)
    core = spread[HALO : HALO + TS]
    across = jnp.asarray(across64, f32)
    waves = jnp.asarray(waves64, f32)
    fixed = jnp.asarray(waves64[REACH : REACH + freqs], f32)
    turn = jnp.asarray(rotation(waves64, freqs), f32)
    total = jnp.sum(source_weight)
    scaled = jnp.tile(pupil / (PAD * PAD), (2 * tiles, 1))

    above = lax.ppermute(mask[TS - HALO :], "tile", [(i, i + 1) for i in range(nt - 1)])
    below = lax.ppermute(mask[:HALO], "tile", [(i + 1, i) for i in range(nt - 1)])
    strip = jnp.concatenate([above, mask, below], axis=0)
    low = mm(mm(spread.T, strip), across)
    zc = mm(waves[:, :GRID], low)
    zs = mm(waves[:, GRID:], low)
    fields = []
    light = jnp.zeros((GRID, tiles * GRID), f32)
    for s in range(own):
        a = source_shift[me * own + s, 0] + REACH
        b = source_shift[me * own + s, 1] + REACH
        w = source_weight[me * own + s]
        c_rows = lax.dynamic_slice_in_dim(zc, a, freqs, 0)
        s_rows = lax.dynamic_slice_in_dim(zs, a, freqs, 0)
        shifted = lax.dynamic_slice_in_dim(waves, b, freqs, 0)
        rows = []
        for c in range(tiles):
            cc = c_rows[:, c * GRID : (c + 1) * GRID]
            ss = s_rows[:, c * GRID : (c + 1) * GRID]
            rows.append(jnp.concatenate([cc, -ss], axis=1))
            rows.append(jnp.concatenate([-ss, -cc], axis=1))
        spec = mm(jnp.concatenate(rows, axis=0), shifted.T) * scaled
        real, imag = halves(mm(spec, fixed), tiles, freqs)
        field = mm(turn, jnp.concatenate([real, imag], axis=0))
        fields.append(field)
        light = light + w * (field[:GRID] * field[:GRID] + field[GRID:] * field[GRID:])
    light = lax.psum(light, "src")
    up = mm(core, light)
    backs = []
    for c in range(tiles):
        fine = mm(up[:, c * GRID : (c + 1) * GRID], core.T)
        slope = resist_slope(fine / total, target[:, c * TS : (c + 1) * TS]) / total
        backs.append(mm(slope, core))
    pull = mm(core.T, jnp.concatenate(backs, axis=1))
    pull = jnp.concatenate([pull, pull], axis=0)
    grid_grad = jnp.zeros((GRID, tiles * GRID), f32)
    for s in range(own):
        a = source_shift[me * own + s, 0] + REACH
        b = source_shift[me * own + s, 1] + REACH
        w = source_weight[me * own + s]
        shift_a = lax.dynamic_slice_in_dim(waves, a, freqs, 0)
        shift_b = lax.dynamic_slice_in_dim(waves, b, freqs, 0)
        u = mm(turn.T, fields[s] * pull * (2.0 * w))
        rows = []
        for c in range(tiles):
            re = u[:freqs, c * GRID : (c + 1) * GRID]
            im = u[freqs:, c * GRID : (c + 1) * GRID]
            rows.append(jnp.concatenate([re, im], axis=1))
            rows.append(jnp.concatenate([im, -re], axis=1))
        back = mm(jnp.concatenate(rows, axis=0), fixed.T) * scaled
        real, imag = halves(mm(back, shift_b), tiles, freqs)
        grid_grad = grid_grad + mm(shift_a[:, :GRID].T, real) - mm(shift_a[:, GRID:].T, imag)
    grid_grad = lax.psum(grid_grad, "src")
    cols = lax.dynamic_slice_in_dim(across, me * width, width, 0)
    full = mm(spread, mm(grid_grad, cols.T))
    upper, inner, lower = full[:HALO], full[HALO : HALO + TS], full[HALO + TS :]
    from_above = lax.ppermute(lower, "tile", [(i, i + 1) for i in range(nt - 1)])
    from_below = lax.ppermute(upper, "tile", [(i + 1, i) for i in range(nt - 1)])
    inner = inner.at[:HALO].add(from_above)
    return inner.at[TS - HALO :].add(from_below)


def solution(mesh):
    placed = (P(("groups", "tile"), None), P(("groups", "tile"), None), P(), P(), P())
    return jax.shard_map(
        shards, mesh=mesh, in_specs=placed, out_specs=P(("groups", "tile"), "src"), check_vma=False
    )
```

profile of v0, /device:TPU:0, one launch (start us, length us, event | category | flops | bytes accessed | tf_op | source)
XLA Modules:
  0.0 207.0 jit_solution(10192906300589848366)
XLA Ops:
  6.6 1.1 fusion.238
  7.7 1.3 collective-permute-start.1
  9.0 3.1 %collective-permute-start = (f32[64,1024]{1,0:T(8,128)S(1)}, f32[64,1024]{1,0:T(8,128)S(1)}, u32[]{:S(2)}, u32[]{:S(2)}) collective-permute-start(f32[64,1024]{1,0:T(8,128)S(1)} %get-tuple-element.29), channel_id=1, source_target_pairs={{0,1},{2,3},{4,5},{6,7},{8,9},{10,11},{12,13},{14,15},{16,17},{18,... | collective-permute-start | bytes 786440 | tf_op jit(solution)/shard_map/ppermute | solution.py:82
  12.0 3.0 %fusion.247 = f32[128,1024]{1,0:T(8,128)S(1)} fusion(f32[512,128]{1,0:T(8,128)} %constant.135, f32[512,1024]{1,0:T(8,128)} %param.14), kind=kOutput, calls=%fused_computation.327 | convolution fusion | flops 805306368 | bytes 2883584 | tf_op jit(solution)/shard_map/dot_general | solution.py:44
  15.1 0.7 constant_dynamic-slice_fusion.4
  23.1 0.7 fusion.246
  23.8 0.6 fusion.248
  24.5 0.7 fusion.10
  25.2 0.6 fusion.249
  31.5 2.4 %fusion.134 = f32[128,256]{0,1:T(8,128)} fusion(f32[256,256]{0,1:T(8,128)S(1)} %fusion.11, f32[256,256]{0,1:T(8,128)S(1)} %fusion.12, f32[256,256]{0,1:T(8,128)S(1)} %fusion.13, f32[]{:T(128)} %bitcast.17, f32[]{:T(128)} %bitcast.9, f32[]{:T(128)} %bitcast.8), kind=kLoop, calls=%fused_computation.152 | loop fusion | flops 458752 | bytes 917516 | tf_op jit(solution)/shard_map/add | solution.py:107
  36.4 70.7 %all-reduce.3.cloned.1.call-done = f32[128,256]{0,1:T(8,128)} async-done(((f32[128,256]{0,1:T(8,128)}), f32[128,256]{0,1:T(8,128)}) %all-reduce.3.cloned.1.call-update) | async-done | bytes 131088 | tf_op jit(solution)/shard_map/psum | solution.py:108
  107.2 1.5 fusion.255
  108.7 1.7 fusion.15
  110.4 1.9 fusion.14
  112.3 1.6 fusion.16
  114.0 1.7 fusion.17
  115.6 1.0 fusion.18
  122.0 1.1 convolution_subtract_fusion
  123.1 69.6 %all-reduce.5.cloned.1.call-done = f32[128,256]{1,0:T(8,128)} async-done(((f32[128,256]{1,0:T(8,128)}), f32[128,256]{1,0:T(8,128)}) %all-reduce.5.cloned.1.call-update) | async-done | bytes 131088 | tf_op jit(solution)/shard_map/psum | solution.py:134
  192.8 1.2 fusion.140
  194.4 1.3 collective-permute-start.2
  195.7 1.3 collective-permute-start.3
  197.1 1.8 collective-permute-done.3
  198.8 1.4 fusion.194
  (92 shorter events, 12.0 us)
Async XLA Ops:
  6.5 17.3 %copy-start.12 = (f32[64,128]{1,0:T(8,128)S(1)}, f32[64,128]{1,0:T(8,128)}, u32[]{:S(2)}) copy-start(f32[64,128]{1,0:T(8,128)} %constant.136) | copy-start | bytes 98308
  6.5 8.5 %copy-start.13 = (f32[64,64]{1,0:T(8,128)S(1)}, f32[64,64]{1,0:T(8,128)}, u32[]{:S(2)}) copy-start(f32[64,64]{1,0:T(8,128)} %param.16) | copy-start | bytes 49156
  6.5 8.5 %copy-start.14 = (s32[24,2]{0,1:T(2,128)S(1)}, s32[24,2]{0,1:T(2,128)}, u32[]{:S(2)}) copy-start(s32[24,2]{0,1:T(2,128)} %param.17) | copy-start | bytes 580
  6.5 16.6 %copy-start.15 = (f32[24]{0:T(128)S(1)}, f32[24]{0:T(128)}, u32[]{:S(2)}) copy-start(f32[24]{0:T(128)} %param.18) | copy-start | bytes 292
  6.5 100.6 %all-reduce.3.cloned.1.call-start = ((), (), s32[]{:S(2)}) async-start(), calls=%async_computation | async-start | bytes 262144 | tf_op jit(solution)/shard_map/psum | solution.py:108
  7.7 16.8 %copy-start.11 = (f32[64,128]{1,0:T(8,128)S(1)}, f32[64,128]{1,0:T(8,128)}, u32[]{:S(2)}) copy-start(f32[64,128]{1,0:T(8,128)} %constant.134) | copy-start | bytes 98308
  7.7 16.1 %collective-permute-start.1 = (f32[64,1024]{1,0:T(8,128)S(1)}, f32[64,1024]{1,0:T(8,128)S(1)}, u32[]{:S(2)}, u32[]{:S(2)}) collective-permute-start(f32[64,1024]{1,0:T(8,128)S(1)} %get-tuple-element.30), channel_id=1, source_target_pairs={{1,0},{3,2},{5,4},{7,6},{9,8},{11,10},{13,12},{15,14},{17,16},{19,... | collective-permute-start | bytes 786440 | tf_op jit(solution)/shard_map/ppermute | solution.py:83
  9.0 15.5 %collective-permute-start = (f32[64,1024]{1,0:T(8,128)S(1)}, f32[64,1024]{1,0:T(8,128)S(1)}, u32[]{:S(2)}, u32[]{:S(2)}) collective-permute-start(f32[64,1024]{1,0:T(8,128)S(1)} %get-tuple-element.29), channel_id=1, source_target_pairs={{0,1},{2,3},{4,5},{6,7},{8,9},{10,11},{12,13},{14,15},{16,17},{18,... | collective-permute-start | bytes 786440 | tf_op jit(solution)/shard_map/ppermute | solution.py:82
  15.0 10.1 %copy-start.2 = (f32[1024,256]{1,0:T(8,128)S(1)}, f32[1024,256]{1,0:T(8,128)}, u32[]{:S(2)}) copy-start(f32[1024,256]{1,0:T(8,128)} %constant.130.clone) | copy-start | bytes 3145732
  23.8 2.0 copy-start.10
  24.4 1.7 copy-start.9
  25.1 1.3 copy-start.1
  25.2 1.7 copy-start.6
  27.3 1.6 copy-start.3
  28.0 2.1 %copy-start.5 = (f32[256,64]{1,0:T(8,128)S(1)}, f32[256,64]{1,0:T(8,128)}, u32[]{:S(2)}) copy-start(f32[256,64]{1,0:T(8,128)} %constant.140) | copy-start | bytes 196612
  29.3 77.9 %copy-start = (f32[512,128]{1,0:T(8,128)S(1)}, f32[512,128]{1,0:T(8,128)}, u32[]{:S(2)}) copy-start(f32[512,128]{1,0:T(8,128)} %constant.135) | copy-start | bytes 786436
  33.9 158.8 %all-reduce.5.cloned.1.call-start = ((), (), s32[]{:S(2)}) async-start(), calls=%async_computation.1 | async-start | bytes 262144 | tf_op jit(solution)/shard_map/psum | solution.py:134
  110.4 1.9 copy-start.16
  113.9 2.7 %copy-start.4 = (f32[256,128]{1,0:T(8,128)S(1)}, f32[256,128]{1,0:T(8,128)}, u32[]{:S(2)}) copy-start(f32[256,128]{1,0:T(8,128)} %constant.133.clone) | copy-start | bytes 393220
  119.5 74.5 %copy-start.8 = (f32[640,128]{1,0:T(8,128)S(1)}, f32[640,128]{1,0:T(8,128)}, u32[]{:S(2)}) copy-start(f32[640,128]{1,0:T(8,128)} %constant.129.clone) | copy-start | bytes 983044
  194.4 2.6 %collective-permute-start.2 = (f32[64,128]{1,0:T(8,128)S(1)}, f32[64,128]{1,0:T(8,128)S(1)}, u32[]{:S(2)}, u32[]{:S(2)}) collective-permute-start(f32[64,128]{1,0:T(8,128)S(1)} %get-tuple-element.32), channel_id=1, source_target_pairs={{0,1},{2,3},{4,5},{6,7},{8,9},{10,11},{12,13},{14,15},{16,17},{18,... | collective-permute-start | bytes 98312 | tf_op jit(solution)/shard_map/ppermute | solution.py:138
  195.7 3.1 %collective-permute-start.3 = (f32[64,128]{1,0:T(8,128)S(1)}, f32[64,128]{1,0:T(8,128)S(1)}, u32[]{:S(2)}, u32[]{:S(2)}) collective-permute-start(f32[64,128]{1,0:T(8,128)S(1)} %get-tuple-element.31), channel_id=1, source_target_pairs={{1,0},{3,2},{5,4},{7,6},{9,8},{11,10},{13,12},{15,14},{17,16},{19,... | collective-permute-start | bytes 98312 | tf_op jit(solution)/shard_map/ppermute | solution.py:139
  197.0 1.8 copy-start.7
Sparse Core Ops, SparseCore 0:
  34.0 73.0 all-reduce.2
  123.2 69.4 all-reduce.4
where the time goes:
time: 208 us; the launch traced here: 207 us
  waiting for transfers between devices  142 us (68%)
  matrix products  27.2 us (13%)
  between operations  23.3 us (11%)
  starting transfers between devices  7.19 us (3%)
  other arithmetic  4.61 us (2%)
  local copies, waits for them, and re-layouts  2.58 us (1%)
    psum x1, waiting for transfers between devices, shards(): light = lax.psum(light, 'src')  70.7 us
    psum x1, waiting for transfers between devices, shards(): grid_grad = lax.psum(grid_grad, 'src')  69.6 us
    dot_general x41, matrix products, mm(): jnp.dot(a, b, precision=exact_mode, preferred_element_type=jnp.float32)  27.2 us
  transfers between devices with their start and end apart: 6, of which 3 were waited for; matrix products, arithmetic and copies ran while one was open for 3% of the time, Pallas kernels for 0%

commit v1 on v0

v1 whole, which is shorter than its diff:
```python
import functools

import numpy as np

import jax
import jax.numpy as jnp
from jax import lax
from jax.experimental import pallas as pl
from jax.experimental.pallas import tpu as pltpu
from jax.sharding import PartitionSpec as P

TS = 512
HALO = 64
PAD = 640
GRID = 128
REACH = 24
CHUNK = 128

MESH = pl.DeviceIdType.MESH
f32, bf16 = jnp.float32, jnp.bfloat16
resist_gain = 25.0
resist_level = 0.25


def tables(freqs, columns):
    pixels = np.arange(PAD)[:, None]
    samples = np.arange(GRID)[None, :] * (PAD // GRID)
    spread = np.ones((PAD, GRID))
    for p in range(1, GRID // 2):
        spread += 2.0 * np.cos(2.0 * np.pi * (p * (pixels - samples) % PAD) / PAD)
    spread /= GRID
    tiles = columns // TS
    across = np.zeros((columns, tiles * GRID))
    for c in range(tiles):
        low, high = max(0, c * TS - HALO), min(columns, c * TS - HALO + PAD)
        across[low:high, c * GRID : (c + 1) * GRID] = spread[low + HALO - c * TS : high + HALO - c * TS]
    bins = np.arange(-freqs // 2 - REACH, freqs // 2 + REACH)[:, None] * np.arange(GRID)[None, :]
    angle = 2.0 * np.pi * (bins % GRID) / GRID
    waves = np.concatenate([np.cos(angle), np.sin(angle)], axis=1)
    return spread, across, waves


def rotation(waves, freqs):
    centre = waves[REACH : REACH + freqs]
    cosine, sine = centre[:, :GRID].T, centre[:, GRID:].T
    return np.block([[cosine, -sine], [sine, cosine]])


def two(array):
    high = array.astype(np.float32).astype(bf16)
    low = (array - high.astype(np.float64)).astype(bf16)
    return np.stack([high, low])


def split(x):
    high = x.astype(bf16)
    return high, (x - high.astype(f32)).astype(bf16)


NN = (((1,), (0,)), ((), ()))
NT = (((1,), (1,)), ((), ()))


def mm(a, b, dims=NN):
    def part(x, y):
        return lax.dot_general(x, y, dims, preferred_element_type=f32)

    return part(a[0], b[0]) + (part(a[0], b[1]) + part(a[1], b[0]))


def pair(ref, *index):
    return ref[(0, *index)], ref[(1, *index)]


def resist_slope(intensity, target):
    printed = jax.nn.sigmoid(resist_gain * (intensity - resist_level))
    return 2.0 * (printed - target) * resist_gain * printed * (1.0 - printed)


def halves(y, tiles, freqs):
    real, imag = [], []
    for c in range(tiles):
        top = y[2 * c * freqs : (2 * c + 1) * freqs]
        low = y[(2 * c + 1) * freqs : (2 * c + 2) * freqs]
        real.append(top[:, :GRID] - low[:, GRID:])
        imag.append(top[:, GRID:] + low[:, :GRID])
    return jnp.concatenate(real, axis=1), jnp.concatenate(imag, axis=1)


def each(count, body):
    if count <= 16:
        for i in range(count):
            body(i)
    else:
        lax.fori_loop(0, count, lambda i, c: (body(i), c)[1], 0)


def kernel(
    n, own, freqs, tiles,
    mask_ref, target_any, pupil_ref, shift_ref, weight_ref,
    core_ref, coret_ref, across_ref, waves_ref, fixed_ref, turn_ref, turnt_ref, edge_ref, edget_ref,
    out_ref,
    target_ref, halo_ref, shifted_ref, low_ref, field_ref, up_ref, pull_ref,
    part_ref, gather_ref, total_ref, rim_ref, rimin_ref,
    target_sem, halo_sem, rim_sem, send_sem, recv_sem,
):
    me = lax.axis_index("src")
    side = lax.axis_index("tile")
    owners = part_ref.shape[1]
    held = part_ref.shape[2]
    width = out_ref.shape[1]
    spans = tiles * GRID

    fetch = pltpu.make_async_copy(target_any, target_ref, target_sem)
    fetch.start()

    barrier = pltpu.get_barrier_semaphore()
    pl.semaphore_signal(barrier, inc=1, device_id={"tile": 1 - side}, device_id_type=MESH)

    def greet(i):
        pl.semaphore_signal(barrier, inc=1, device_id={"src": lax.rem(me + i + 1, n)}, device_id_type=MESH)

    each(n - 1, greet)

    span = waves_ref.shape[1]
    gap = lax.broadcasted_iota(jnp.int32, (freqs, span), 1) - lax.broadcasted_iota(jnp.int32, (freqs, span), 0)
    for s in range(own):
        for axis in (0, 1):
            picks = jnp.where(gap == shift_ref[me * own + s, axis] + REACH, 1.0, 0.0).astype(bf16)
            shifted_ref[s, axis] = lax.dot_general(picks, waves_ref[0], NN, preferred_element_type=f32) + lax.dot_general(
                picks, waves_ref[1], NN, preferred_element_type=f32
            )

    low_ref[...] = jnp.zeros_like(low_ref)

    def project(left, source, height):
        def block(i, carry):
            at = pl.multiple_of(i * 256, 256)
            rows = mm(left, split(source[0:height, pl.ds(at, 256)]))
            low_ref[...] += mm(split(rows), pair(across_ref, pl.ds(at, 256)))
            return carry

        lax.fori_loop(0, mask_ref.shape[1] // 256, block, 0)

    pl.semaphore_wait(barrier, n)
    first = pl.multiple_of((TS - HALO) * (1 - side), HALO)
    halo = pltpu.make_async_remote_copy(
        src_ref=mask_ref.at[pl.ds(first, HALO)],
        dst_ref=halo_ref,
        send_sem=halo_sem.at[0],
        recv_sem=halo_sem.at[1],
        device_id={"tile": 1 - side},
        device_id_type=MESH,
    )
    halo.start()
    project(pair(coret_ref), mask_ref, TS)
    halo.wait_recv()
    project(pair(edget_ref, side), halo_ref, HALO)

    low = split(low_ref[...])

    def turns():
        return jnp.concatenate(
            [shifted_ref[s, 0, :, half * GRID : (half + 1) * GRID] for s in range(own) for half in (0, 1)], axis=0
        )

    spun = mm(split(turns()), low)
    scaled = pupil_ref[...] * (1.0 / (PAD * PAD))
    scaled = jnp.concatenate([scaled] * (2 * tiles), axis=0)
    fixed = pair(fixed_ref)

    light = jnp.zeros((GRID, spans), f32)
    for s in range(own):
        w = weight_ref[me * own + s]
        c_rows = spun[2 * s * freqs : (2 * s + 1) * freqs]
        s_rows = spun[(2 * s + 1) * freqs : (2 * s + 2) * freqs]
        rows = []
        for c in range(tiles):
            cc = c_rows[:, c * GRID : (c + 1) * GRID]
            ss = s_rows[:, c * GRID : (c + 1) * GRID]
            rows.append(jnp.concatenate([cc, -ss], axis=1))
            rows.append(jnp.concatenate([-ss, -cc], axis=1))
        spec = mm(split(jnp.concatenate(rows, axis=0)), split(shifted_ref[s, 1]), NT) * scaled
        real, imag = halves(mm(split(spec), fixed), tiles, freqs)
        field = mm(pair(turn_ref), split(jnp.concatenate([real, imag], axis=0)))
        field_ref[s] = field
        light = light + w * (field[:GRID] * field[:GRID] + field[GRID:] * field[GRID:])

    def summed(k, value):
        for p in range(owners):
            part_ref[k, p] = value[p * held : (p + 1) * held]

        def owning(condition, action):
            if owners == n:
                action()
            else:
                pl.when(condition)(action)

        def scatter(peer):
            return pltpu.make_async_remote_copy(
                src_ref=part_ref.at[k, lax.rem(peer, owners)],
                dst_ref=gather_ref.at[k, me],
                send_sem=send_sem.at[2 * k, peer],
                recv_sem=recv_sem.at[2 * k, me],
                device_id={"src": peer},
                device_id_type=MESH,
            )

        def arrival(peer):
            return pltpu.make_async_remote_copy(
                src_ref=part_ref.at[k, 0],
                dst_ref=gather_ref.at[k, peer],
                send_sem=send_sem.at[2 * k, peer],
                recv_sem=recv_sem.at[2 * k, peer],
                device_id={"src": peer},
                device_id_type=MESH,
            )

        def share(peer):
            return pltpu.make_async_remote_copy(
                src_ref=total_ref.at[k, lax.rem(me, owners)],
                dst_ref=total_ref.at[k, lax.rem(me, owners)],
                send_sem=send_sem.at[2 * k + 1, peer],
                recv_sem=recv_sem.at[2 * k + 1, me],
                device_id={"src": peer},
                device_id_type=MESH,
            )

        def shared(peer):
            return pltpu.make_async_remote_copy(
                src_ref=total_ref.at[k, lax.rem(peer, owners)],
                dst_ref=total_ref.at[k, lax.rem(peer, owners)],
                send_sem=send_sem.at[2 * k + 1, peer],
                recv_sem=recv_sem.at[2 * k + 1, peer],
                device_id={"src": peer},
                device_id_type=MESH,
            )

        def other(i):
            return lax.rem(me + i + 1, n)

        each(n - 1, lambda i: owning(other(i) < owners, lambda: scatter(other(i)).start()))

        def add_up():
            each(n - 1, lambda i: arrival(other(i)).wait_recv())
            gather_ref[k, me] = part_ref[k, lax.rem(me, owners)]
            block = gather_ref[k, 0]
            if n <= 16:
                for p in range(1, n):
                    block = block + gather_ref[k, p]
            else:
                block = lax.fori_loop(1, n, lambda p, t: t + gather_ref[k, p], block)
            total_ref[k, lax.rem(me, owners)] = block
            each(n - 1, lambda i: share(other(i)).start())

        owning(me < owners, add_up)
        each(n - 1, lambda i: owning(other(i) < owners, lambda: shared(other(i)).wait_recv()))
        each(n - 1, lambda i: owning(other(i) < owners, lambda: scatter(other(i)).wait_send()))
        owning(me < owners, lambda: each(n - 1, lambda i: share(other(i)).wait_send()))
        return jnp.concatenate([total_ref[k, p] for p in range(owners)], axis=0)

    light = split(summed(0, light))

    weight = weight_ref[0]
    for s in range(1, n * own):
        weight = weight + weight_ref[s]
    inverse = 1.0 / jnp.full((1, TS), weight, f32)
    fetch.wait()
    core = pair(core_ref)
    coret = pair(coret_ref)
    up_ref[...] = mm(core, light)
    pull_ref[...] = jnp.zeros_like(pull_ref)

    def resist(i, carry):
        at = pl.multiple_of(i * CHUNK, CHUNK)
        backs = []
        for c in range(tiles):
            fine = mm(split(up_ref[pl.ds(at, CHUNK), c * GRID : (c + 1) * GRID]), coret)
            slope = resist_slope(fine * inverse, target_ref[pl.ds(at, CHUNK), c * TS : (c + 1) * TS]) * inverse
            backs.append(mm(split(slope), core))
        rows = jnp.concatenate(backs, axis=1)
        pull_ref[...] += mm(pair(coret_ref, slice(None), pl.ds(at, CHUNK)), split(rows))
        return carry

    lax.fori_loop(0, TS // CHUNK, resist, 0)

    pull = jnp.concatenate([pull_ref[...]] * 2, axis=0)
    lows = []
    for s in range(own):
        w = weight_ref[me * own + s]
        u = mm(pair(turnt_ref), split(field_ref[s] * pull * (2.0 * w)))
        rows = []
        for c in range(tiles):
            re = u[:freqs, c * GRID : (c + 1) * GRID]
            im = u[freqs:, c * GRID : (c + 1) * GRID]
            rows.append(jnp.concatenate([re, im], axis=1))
            rows.append(jnp.concatenate([im, -re], axis=1))
        back = mm(split(jnp.concatenate(rows, axis=0)), fixed, NT) * scaled
        real, imag = halves(mm(split(back), split(shifted_ref[s, 1])), tiles, freqs)
        lows += [real, -imag]
    lead = split(turns().T)
    grid_grad = mm(lead, split(jnp.concatenate(lows, axis=0)))

    grid_grad = split(summed(1, grid_grad))
    at = pl.multiple_of(me * width, width)
    block = split(mm(grid_grad, pair(across_ref, pl.ds(at, width)), NT))
    rim_ref[...] = mm(pair(edge_ref, side), block)
    rim = pltpu.make_async_remote_copy(
        src_ref=rim_ref,
        dst_ref=rimin_ref,
        send_sem=rim_sem.at[0],
        recv_sem=rim_sem.at[1],
        device_id={"tile": 1 - side},
        device_id_type=MESH,
    )
    rim.start()
    out_ref[...] = mm(core, block)
    rim.wait_recv()
    out_ref[pl.ds(first, HALO), :] += rimin_ref[...]
    halo.wait_send()
    rim.wait_send()


def shards(mask, target, pupil, source_shift, source_weight):
    n = lax.axis_size("src")
    assert lax.axis_size("tile") == 2
    own = source_shift.shape[0] // n
    freqs = pupil.shape[0]
    columns = mask.shape[1]
    tiles = columns // TS
    width = columns // n
    owners = min(n, GRID // 8)
    spans = tiles * GRID
    spread, across, waves = tables(freqs, columns)
    core = spread[HALO : HALO + TS]
    edges = np.stack([spread[HALO + TS :], spread[:HALO]])
    turn = rotation(waves, freqs)
    constants = [
        two(core), two(core.T), two(across), two(waves),
        two(waves[REACH : REACH + freqs]), two(turn), two(turn.T), two(edges), two(edges.transpose(0, 2, 1)),
    ]
    vmem = pl.BlockSpec(memory_space=pltpu.VMEM)
    smem = pl.BlockSpec(memory_space=pltpu.SMEM)
    return pl.pallas_call(
        functools.partial(kernel, n, own, freqs, tiles),
        out_shape=jax.ShapeDtypeStruct((TS, width), f32),
        in_specs=[vmem, pl.BlockSpec(memory_space=pl.ANY), vmem, smem, smem] + [vmem] * len(constants),
        out_specs=vmem,
        scratch_shapes=[
            pltpu.VMEM((TS, columns), f32),
            pltpu.VMEM((HALO, columns), f32),
            pltpu.VMEM((own, 2, freqs, 2 * GRID), f32),
            pltpu.VMEM((GRID, spans), f32),
            pltpu.VMEM((own, 2 * GRID, spans), f32),
            pltpu.VMEM((TS, spans), f32),
            pltpu.VMEM((GRID, spans), f32),
            pltpu.VMEM((2, owners, GRID // owners, spans), f32),
            pltpu.VMEM((2, n, GRID // owners, spans), f32),
            pltpu.VMEM((2, owners, GRID // owners, spans), f32),
            pltpu.VMEM((HALO, width), f32),
            pltpu.VMEM((HALO, width), f32),
            pltpu.SemaphoreType.DMA,
            pltpu.SemaphoreType.DMA((2,)),
            pltpu.SemaphoreType.DMA((2,)),
            pltpu.SemaphoreType.DMA((4, n)),
            pltpu.SemaphoreType.DMA((4, n)),
        ],
        compiler_params=pltpu.CompilerParams(
            collective_id=0, has_side_effects=True, vmem_limit_bytes=60 * 1024 * 1024
        ),
    )(mask, target, pupil, source_shift, source_weight, *[jnp.asarray(c) for c in constants])


def solution(mesh):
    placed = (P(("groups", "tile"), None), P(("groups", "tile"), None), P(), P(), P())
    return jax.shard_map(
        shards, mesh=mesh, in_specs=placed, out_specs=P(("groups", "tile"), "src"), check_vma=False
    )
```

time: 208 us -> 45.6 us (0.22)
  waiting for transfers between devices: 142 us -> 0 us
  Pallas kernels: 0 us -> 42.4 us
  matrix products: 27.2 us -> 0 us
  between operations: 23.3 us -> 0.01 us
  starting transfers between devices: 7.19 us -> 0 us
  other arithmetic: 4.61 us -> 0 us
    psum x2 -> x0, waiting for transfers between devices: 140 us -> none  [the longest x1 70.7 us: shards(): light = lax.psum(light, 'src')]
    pallas_call x0 -> x1, Pallas kernels: none -> 42.4 us  [shards(): pl.pallas_call(functools.partial(kernel, n, own, freqs, tiles), out_shape...]
    dot_general x41 -> x0, matrix products: 27.2 us -> none  [mm(): jnp.dot(a, b, precision=exact_mode, preferred_element_type=jnp.float32)]
    ppermute x4 -> x0, starting transfers between devices: 6.93 us -> none  [the longest x1 3.06 us: shards(): lax.ppermute(mask[TS - HALO:], 'tile', [(i, i + 1) for i in range(nt - 1)])]
    unnamed x34 -> x2, local copies, waits for them, and re-layouts: 0.1 us -> 3.03 us
    add x7 -> x0, other arithmetic: 2.54 us -> none  [the longest x1 2.44 us: shards(): light + w * (field[:GRID] * field[:GRID] + field[GRID:] * field[GRID:])]
  transfers between devices with their start and end apart: 6 -> 0, of which waited for: 3 -> 0; matrix products, arithmetic and copies ran while one was open for 3% -> 0% of each run, Pallas kernels for 0% -> 0%
where the time goes in v1:
time: 45.6 us; the launch traced here: 45.5 us
  Pallas kernels  42.4 us (93%)
  local copies, waits for them, and re-layouts  3.03 us (7%)
    pallas_call x1, Pallas kernels, shards(): pl.pallas_call(functools.partial(kernel, n, own, freqs, tiles), out_shape...  42.4 us
    unnamed x2, local copies, waits for them, and re-layouts  3.03 us

profile of v1, /device:TPU:0, one launch (start us, length us, event | category | flops | bytes accessed | tf_op | source)
XLA Modules:
  0.0 45.5 jit_solution(4197246230934882303)
XLA Ops:
  0.0 1.4 %copy.15.shift_ref = s32[24,2]{1,0:T(8,128)} copy(s32[24,2]{0,1:T(2,128)} %param.17) | data formatting | bytes 384 | tf_op args[3]
  1.4 42.4 %shard_map.136 = f32[512,128]{1,0:T(8,128)} custom-call(f32[512,1024]{1,0:T(8,128)} %mask_ref.1, f32[512,1024]{1,0:T(8,128)} %target_any.1, f32[64,64]{1,0:T(8,128)} %pupil_ref.1, s32[24,2]{1,0:T(8,128)} %copy.15.shift_ref, f32[24]{0:T(128)} %weight_ref.1, bf16[2,512,128]{2,1,0:T(8,128)(2,1)} %constant.18.clone.core_ref, ...), custom_call_target="tpu_custom_call" | custom-call | tf_op jit(solution)/shard_map/pallas_call | solution.py:344
  43.8 1.7 %copy.17 = f32[512,128]{1,0:T(8,128)} copy(f32[512,128]{1,0:T(8,128)} %shard_map.136) | data formatting | bytes 524288

commit v2 on v1

--- a/solution.py
+++ b/solution.py
@@ -97,12 +97,13 @@
 
 def kernel(
     n, own, freqs, tiles,
-    mask_ref, target_any, pupil_ref, shift_ref, weight_ref,
+    mask_any, target_any, pupil_ref, shift_ref, weight_ref,
+    core_any, coret_any, across_any, waves_any, fixed_any, turn_any, turnt_any, edge_any, edget_any,
+    out_ref,
     core_ref, coret_ref, across_ref, waves_ref, fixed_ref, turn_ref, turnt_ref, edge_ref, edget_ref,
-    out_ref,
-    target_ref, halo_ref, shifted_ref, low_ref, field_ref, up_ref, pull_ref,
+    mask_ref, target_ref, halo_ref, shifted_ref, low_ref, field_ref, up_ref, pull_ref,
     part_ref, gather_ref, total_ref, rim_ref, rimin_ref,
-    target_sem, halo_sem, rim_sem, send_sem, recv_sem,
+    load_sem, halo_sem, rim_sem, send_sem, recv_sem,
 ):
     me = lax.axis_index("src")
     side = lax.axis_index("tile")
@@ -111,9 +112,6 @@
     width = out_ref.shape[1]
     spans = tiles * GRID
 
-    fetch = pltpu.make_async_copy(target_any, target_ref, target_sem)
-    fetch.start()
-
     barrier = pltpu.get_barrier_semaphore()
     pl.semaphore_signal(barrier, inc=1, device_id={"tile": 1 - side}, device_id_type=MESH)
 
@@ -121,12 +119,22 @@
         pl.semaphore_signal(barrier, inc=1, device_id={"src": lax.rem(me + i + 1, n)}, device_id_type=MESH)
 
     each(n - 1, greet)
+
+    places = [
+        (waves_any, waves_ref), (mask_any, mask_ref), (coret_any, coret_ref), (across_any, across_ref),
+        (edget_any, edget_ref), (fixed_any, fixed_ref), (turn_any, turn_ref), (target_any, target_ref),
+        (core_any, core_ref), (turnt_any, turnt_ref), (edge_any, edge_ref),
+    ]
+    loads = [pltpu.make_async_copy(source, place, load_sem.at[i]) for i, (source, place) in enumerate(places)]
+    for load in loads:
+        load.start()
+    loads[0].wait()
 
     span = waves_ref.shape[1]
     gap = lax.broadcasted_iota(jnp.int32, (freqs, span), 1) - lax.broadcasted_iota(jnp.int32, (freqs, span), 0)
     for s in range(own):
         for axis in (0, 1):
-            picks = jnp.where(gap == shift_ref[me * own + s, axis] + REACH, 1.0, 0.0).astype(bf16)
+            picks = jnp.where(gap == shift_ref[axis, me * own + s] + REACH, 1.0, 0.0).astype(bf16)
             shifted_ref[s, axis] = lax.dot_general(picks, waves_ref[0], NN, preferred_element_type=f32) + lax.dot_general(
                 picks, waves_ref[1], NN, preferred_element_type=f32
             )
@@ -145,7 +153,7 @@
     pl.semaphore_wait(barrier, n)
     first = pl.multiple_of((TS - HALO) * (1 - side), HALO)
     halo = pltpu.make_async_remote_copy(
-        src_ref=mask_ref.at[pl.ds(first, HALO)],
+        src_ref=mask_any.at[pl.ds(first, HALO)],
         dst_ref=halo_ref,
         send_sem=halo_sem.at[0],
         recv_sem=halo_sem.at[1],
@@ -153,7 +161,11 @@
         device_id_type=MESH,
     )
     halo.start()
+    for load in loads[1:4]:
+        load.wait()
     project(pair(coret_ref), mask_ref, TS)
+    for load in loads[4:7]:
+        load.wait()
     halo.wait_recv()
     project(pair(edget_ref, side), halo_ref, HALO)
 
@@ -265,7 +277,8 @@
     for s in range(1, n * own):
         weight = weight + weight_ref[s]
     inverse = 1.0 / jnp.full((1, TS), weight, f32)
-    fetch.wait()
+    for load in loads[7:]:
+        load.wait()
     core = pair(core_ref)
     coret = pair(coret_ref)
     up_ref[...] = mm(core, light)
@@ -339,14 +352,16 @@
         two(core), two(core.T), two(across), two(waves),
         two(waves[REACH : REACH + freqs]), two(turn), two(turn.T), two(edges), two(edges.transpose(0, 2, 1)),
     ]
+    hbm = pl.BlockSpec(memory_space=pl.ANY)
     vmem = pl.BlockSpec(memory_space=pltpu.VMEM)
     smem = pl.BlockSpec(memory_space=pltpu.SMEM)
     return pl.pallas_call(
         functools.partial(kernel, n, own, freqs, tiles),
         out_shape=jax.ShapeDtypeStruct((TS, width), f32),
-        in_specs=[vmem, pl.BlockSpec(memory_space=pl.ANY), vmem, smem, smem] + [vmem] * len(constants),
+        in_specs=[hbm, hbm, vmem, smem, smem] + [hbm] * len(constants),
         out_specs=vmem,
-        scratch_shapes=[
+        scratch_shapes=[pltpu.VMEM(c.shape, c.dtype) for c in constants] + [
+            pltpu.VMEM((TS, columns), f32),
             pltpu.VMEM((TS, columns), f32),
             pltpu.VMEM((HALO, columns), f32),
             pltpu.VMEM((own, 2, freqs, 2 * GRID), f32),
@@ -359,7 +374,7 @@
             pltpu.VMEM((2, owners, GRID // owners, spans), f32),
             pltpu.VMEM((HALO, width), f32),
             pltpu.VMEM((HALO, width), f32),
-            pltpu.SemaphoreType.DMA,
+            pltpu.SemaphoreType.DMA((2 + len(constants),)),
             pltpu.SemaphoreType.DMA((2,)),
             pltpu.SemaphoreType.DMA((2,)),
             pltpu.SemaphoreType.DMA((4, n)),
@@ -368,7 +383,7 @@
         compiler_params=pltpu.CompilerParams(
             collective_id=0, has_side_effects=True, vmem_limit_bytes=60 * 1024 * 1024
         ),
-    )(mask, target, pupil, source_shift, source_weight, *[jnp.asarray(c) for c in constants])
+    )(mask, target, pupil, source_shift.T, source_weight, *[jnp.asarray(c) for c in constants])
 
 
 def solution(mesh):

time: 45.6 us -> 43.8 us (0.961)
  local copies, waits for them, and re-layouts: 3.03 us -> 1.67 us
  Pallas kernels: 42.4 us -> 41.9 us
    unnamed x2 -> x1, local copies, waits for them, and re-layouts: 3.03 us -> 1.67 us
    pallas_call x1, Pallas kernels: 42.4 us -> 41.9 us  [shards(): pl.pallas_call(functools.partial(kernel, n, own, freqs, tiles), out_shape...]
where the time goes in v2:
time: 43.8 us; the launch traced here: 43.6 us
  Pallas kernels  41.9 us (96%)
  local copies, waits for them, and re-layouts  1.67 us (4%)
    pallas_call x1, Pallas kernels, shards(): pl.pallas_call(functools.partial(kernel, n, own, freqs, tiles), out_shape...  41.9 us
    unnamed x1, local copies, waits for them, and re-layouts  1.67 us

profile of v2, /device:TPU:0, one launch (start us, length us, event | category | flops | bytes accessed | tf_op | source)
XLA Modules:
  0.0 43.6 jit_solution(13500073564227462852)
XLA Ops:
  0.0 41.9 %shard_map.136 = f32[512,128]{1,0:T(8,128)} custom-call(f32[512,1024]{1,0:T(8,128)} %mask_any.1, f32[512,1024]{1,0:T(8,128)} %target_any.1, f32[64,64]{1,0:T(8,128)} %pupil_ref.1, s32[2,24]{1,0:T(2,128)} %bitcast.1, f32[24]{0:T(128)} %weight_ref.1, bf16[2,512,128]{2,1,0:T(8,128)(2,1)} %constant.18.clone.core_any, ...), custom_call_target="tpu_custom_call" | custom-call | tf_op jit(solution)/shard_map/pallas_call | solution.py:358
  41.9 1.7 %copy.16 = f32[512,128]{1,0:T(8,128)} copy(f32[512,128]{1,0:T(8,128)} %shard_map.136) | data formatting | bytes 524288

commit v3 on v2

--- a/solution.py
+++ b/solution.py
@@ -14,7 +14,7 @@
 PAD = 640
 GRID = 128
 REACH = 24
-CHUNK = 128
+CHUNK = 256
 
 MESH = pl.DeviceIdType.MESH
 f32, bf16 = jnp.float32, jnp.bfloat16
@@ -77,14 +77,14 @@
     return 2.0 * (printed - target) * resist_gain * printed * (1.0 - printed)
 
 
-def halves(y, tiles, freqs):
+def halves(y, count, freqs):
     real, imag = [], []
-    for c in range(tiles):
+    for c in range(count):
         top = y[2 * c * freqs : (2 * c + 1) * freqs]
         low = y[(2 * c + 1) * freqs : (2 * c + 2) * freqs]
         real.append(top[:, :GRID] - low[:, GRID:])
         imag.append(top[:, GRID:] + low[:, :GRID])
-    return jnp.concatenate(real, axis=1), jnp.concatenate(imag, axis=1)
+    return real, imag
 
 
 def each(count, body):
@@ -110,7 +110,6 @@
     owners = part_ref.shape[1]
     held = part_ref.shape[2]
     width = out_ref.shape[1]
-    spans = tiles * GRID
 
     barrier = pltpu.get_barrier_semaphore()
     pl.semaphore_signal(barrier, inc=1, device_id={"tile": 1 - side}, device_id_type=MESH)
@@ -178,30 +177,32 @@
 
     spun = mm(split(turns()), low)
     scaled = pupil_ref[...] * (1.0 / (PAD * PAD))
-    scaled = jnp.concatenate([scaled] * (2 * tiles), axis=0)
+    scaled = jnp.concatenate([scaled] * (2 * own), axis=0)
     fixed = pair(fixed_ref)
 
-    light = jnp.zeros((GRID, spans), f32)
-    for s in range(own):
-        w = weight_ref[me * own + s]
-        c_rows = spun[2 * s * freqs : (2 * s + 1) * freqs]
-        s_rows = spun[(2 * s + 1) * freqs : (2 * s + 2) * freqs]
-        rows = []
-        for c in range(tiles):
-            cc = c_rows[:, c * GRID : (c + 1) * GRID]
-            ss = s_rows[:, c * GRID : (c + 1) * GRID]
-            rows.append(jnp.concatenate([cc, -ss], axis=1))
-            rows.append(jnp.concatenate([-ss, -cc], axis=1))
-        spec = mm(split(jnp.concatenate(rows, axis=0)), split(shifted_ref[s, 1]), NT) * scaled
-        real, imag = halves(mm(split(spec), fixed), tiles, freqs)
-        field = mm(pair(turn_ref), split(jnp.concatenate([real, imag], axis=0)))
-        field_ref[s] = field
-        light = light + w * (field[:GRID] * field[:GRID] + field[GRID:] * field[GRID:])
-
-    def summed(k, value):
-        for p in range(owners):
-            part_ref[k, p] = value[p * held : (p + 1) * held]
-
+    weights = [weight_ref[me * own + s] for s in range(own)]
+
+    def image(c):
+        lanes = slice(c * GRID, (c + 1) * GRID)
+        specs = []
+        for s in range(own):
+            cc = spun[2 * s * freqs : (2 * s + 1) * freqs, lanes]
+            ss = spun[(2 * s + 1) * freqs : (2 * s + 2) * freqs, lanes]
+            rows = [jnp.concatenate([cc, -ss], axis=1), jnp.concatenate([-ss, -cc], axis=1)]
+            specs.append(mm(split(jnp.concatenate(rows, axis=0)), split(shifted_ref[s, 1]), NT))
+        spec = jnp.concatenate(specs, axis=0) * scaled
+        real, imag = halves(mm(split(spec), fixed), own, freqs)
+        stack = jnp.concatenate([jnp.concatenate(real, axis=1), jnp.concatenate(imag, axis=1)], axis=0)
+        field = mm(pair(turn_ref), split(stack))
+        field_ref[c] = field
+        light = jnp.zeros((GRID, GRID), f32)
+        for s in range(own):
+            re = field[:GRID, s * GRID : (s + 1) * GRID]
+            im = field[GRID:, s * GRID : (s + 1) * GRID]
+            light = light + weights[s] * (re * re + im * im)
+        return light
+
+    def owning_sum(k):
         def owning(condition, action):
             if owners == n:
                 action()
@@ -251,7 +252,10 @@
         def other(i):
             return lax.rem(me + i + 1, n)
 
-        each(n - 1, lambda i: owning(other(i) < owners, lambda: scatter(other(i)).start()))
+        def begin(value):
+            for p in range(owners):
+                part_ref[k, p] = value[p * held : (p + 1) * held]
+            each(n - 1, lambda i: owning(other(i) < owners, lambda: scatter(other(i)).start()))
 
         def add_up():
             each(n - 1, lambda i: arrival(other(i)).wait_recv())
@@ -265,13 +269,22 @@
             total_ref[k, lax.rem(me, owners)] = block
             each(n - 1, lambda i: share(other(i)).start())
 
-        owning(me < owners, add_up)
-        each(n - 1, lambda i: owning(other(i) < owners, lambda: shared(other(i)).wait_recv()))
-        each(n - 1, lambda i: owning(other(i) < owners, lambda: scatter(other(i)).wait_send()))
-        owning(me < owners, lambda: each(n - 1, lambda i: share(other(i)).wait_send()))
-        return jnp.concatenate([total_ref[k, p] for p in range(owners)], axis=0)
-
-    light = split(summed(0, light))
+        def middle():
+            owning(me < owners, add_up)
+
+        def end():
+            each(n - 1, lambda i: owning(other(i) < owners, lambda: shared(other(i)).wait_recv()))
+            return jnp.concatenate([total_ref[k, p] for p in range(owners)], axis=0)
+
+        def drain():
+            each(n - 1, lambda i: owning(other(i) < owners, lambda: scatter(other(i)).wait_send()))
+            owning(me < owners, lambda: each(n - 1, lambda i: share(other(i)).wait_send()))
+
+        return begin, middle, end, drain
+
+    sums = [owning_sum(k) for k in range(2 * tiles)]
+    for c in range(tiles):
+        sums[c][0](image(c))
 
     weight = weight_ref[0]
     for s in range(1, n * own):
@@ -281,40 +294,48 @@
         load.wait()
     core = pair(core_ref)
     coret = pair(coret_ref)
-    up_ref[...] = mm(core, light)
-    pull_ref[...] = jnp.zeros_like(pull_ref)
-
-    def resist(i, carry):
-        at = pl.multiple_of(i * CHUNK, CHUNK)
-        backs = []
-        for c in range(tiles):
-            fine = mm(split(up_ref[pl.ds(at, CHUNK), c * GRID : (c + 1) * GRID]), coret)
+    lead = split(turns().T)
+    for c in range(tiles):
+        sums[c][1]()
+
+    def pulled(c, light):
+        up_ref[c] = mm(core, split(light))
+        pull_ref[c] = jnp.zeros((GRID, GRID), f32)
+
+        def resist(i, carry):
+            at = pl.multiple_of(i * CHUNK, CHUNK)
+            fine = mm(split(up_ref[c, pl.ds(at, CHUNK), :]), coret)
             slope = resist_slope(fine * inverse, target_ref[pl.ds(at, CHUNK), c * TS : (c + 1) * TS]) * inverse
-            backs.append(mm(split(slope), core))
-        rows = jnp.concatenate(backs, axis=1)
-        pull_ref[...] += mm(pair(coret_ref, slice(None), pl.ds(at, CHUNK)), split(rows))
-        return carry
-
-    lax.fori_loop(0, TS // CHUNK, resist, 0)
-
-    pull = jnp.concatenate([pull_ref[...]] * 2, axis=0)
-    lows = []
-    for s in range(own):
-        w = weight_ref[me * own + s]
-        u = mm(pair(turnt_ref), split(field_ref[s] * pull * (2.0 * w)))
+            rows = mm(split(slope), core)
+            pull_ref[c] += mm(pair(coret_ref, slice(None), pl.ds(at, CHUNK)), split(rows))
+            return carry
+
+        lax.fori_loop(0, TS // CHUNK, resist, 0)
+        return pull_ref[c]
+
+    def gradient(c, pull):
+        pull = jnp.concatenate([pull] * 2, axis=0)
+        pull = jnp.concatenate([pull * (2.0 * w) for w in weights], axis=1)
+        u = mm(pair(turnt_ref), split(field_ref[c] * pull))
         rows = []
-        for c in range(tiles):
-            re = u[:freqs, c * GRID : (c + 1) * GRID]
-            im = u[freqs:, c * GRID : (c + 1) * GRID]
+        for s in range(own):
+            re = u[:freqs, s * GRID : (s + 1) * GRID]
+            im = u[freqs:, s * GRID : (s + 1) * GRID]
             rows.append(jnp.concatenate([re, im], axis=1))
             rows.append(jnp.concatenate([im, -re], axis=1))
         back = mm(split(jnp.concatenate(rows, axis=0)), fixed, NT) * scaled
-        real, imag = halves(mm(split(back), split(shifted_ref[s, 1])), tiles, freqs)
-        lows += [real, -imag]
-    lead = split(turns().T)
-    grid_grad = mm(lead, split(jnp.concatenate(lows, axis=0)))
-
-    grid_grad = split(summed(1, grid_grad))
+        lows = []
+        for s in range(own):
+            wide = mm(split(back[2 * s * freqs : 2 * (s + 1) * freqs]), split(shifted_ref[s, 1]))
+            real, imag = halves(wide, 1, freqs)
+            lows += [real[0], -imag[0]]
+        return mm(lead, split(jnp.concatenate(lows, axis=0)))
+
+    for c in range(tiles):
+        sums[tiles + c][0](gradient(c, pulled(c, sums[c][2]())))
+    for c in range(tiles):
+        sums[tiles + c][1]()
+    grid_grad = split(jnp.concatenate([sums[tiles + c][2]() for c in range(tiles)], axis=1))
     at = pl.multiple_of(me * width, width)
     block = split(mm(grid_grad, pair(across_ref, pl.ds(at, width)), NT))
     rim_ref[...] = mm(pair(edge_ref, side), block)
@@ -330,6 +351,8 @@
     out_ref[...] = mm(core, block)
     rim.wait_recv()
     out_ref[pl.ds(first, HALO), :] += rimin_ref[...]
+    for one in sums:
+        one[3]()
     halo.wait_send()
     rim.wait_send()
 
@@ -366,19 +389,19 @@
             pltpu.VMEM((HALO, columns), f32),
             pltpu.VMEM((own, 2, freqs, 2 * GRID), f32),
             pltpu.VMEM((GRID, spans), f32),
-            pltpu.VMEM((own, 2 * GRID, spans), f32),
-            pltpu.VMEM((TS, spans), f32),
-            pltpu.VMEM((GRID, spans), f32),
-            pltpu.VMEM((2, owners, GRID // owners, spans), f32),
-            pltpu.VMEM((2, n, GRID // owners, spans), f32),
-            pltpu.VMEM((2, owners, GRID // owners, spans), f32),
+            pltpu.VMEM((tiles, 2 * GRID, own * GRID), f32),
+            pltpu.VMEM((tiles, TS, GRID), f32),
+            pltpu.VMEM((tiles, GRID, GRID), f32),
+            pltpu.VMEM((2 * tiles, owners, GRID // owners, GRID), f32),
+            pltpu.VMEM((2 * tiles, n, GRID // owners, GRID), f32),
+            pltpu.VMEM((2 * tiles, owners, GRID // owners, GRID), f32),
             pltpu.VMEM((HALO, width), f32),
             pltpu.VMEM((HALO, width), f32),
             pltpu.SemaphoreType.DMA((2 + len(constants),)),
             pltpu.SemaphoreType.DMA((2,)),
             pltpu.SemaphoreType.DMA((2,)),
-            pltpu.SemaphoreType.DMA((4, n)),
-            pltpu.SemaphoreType.DMA((4, n)),
+            pltpu.SemaphoreType.DMA((4 * tiles, n)),
+            pltpu.SemaphoreType.DMA((4 * tiles, n)),
         ],
         compiler_params=pltpu.CompilerParams(
             collective_id=0, has_side_effects=True, vmem_limit_bytes=60 * 1024 * 1024

time: 43.8 us -> 42.3 us (0.966)
  Pallas kernels: 41.9 us -> 40.4 us
    pallas_call x1, Pallas kernels: 41.9 us -> 40.4 us  [shards(): pl.pallas_call(functools.partial(kernel, n, own, freqs, tiles), out_shape...]
where the time goes in v3:
time: 42.3 us; the launch traced here: 42.1 us
  Pallas kernels  40.4 us (96%)
  local copies, waits for them, and re-layouts  1.67 us (4%)
    pallas_call x1, Pallas kernels, shards(): pl.pallas_call(functools.partial(kernel, n, own, freqs, tiles), out_shape...  40.4 us
    unnamed x1, local copies, waits for them, and re-layouts  1.67 us

profile of v3, /device:TPU:0, one launch (start us, length us, event | category | flops | bytes accessed | tf_op | source)
XLA Modules:
  0.0 42.1 jit_solution(9878127212110628404)
XLA Ops:
  0.0 40.4 %shard_map.136 = f32[512,128]{1,0:T(8,128)} custom-call(f32[512,1024]{1,0:T(8,128)} %mask_any.1, f32[512,1024]{1,0:T(8,128)} %target_any.1, f32[64,64]{1,0:T(8,128)} %pupil_ref.1, s32[2,24]{1,0:T(2,128)} %bitcast.1, f32[24]{0:T(128)} %weight_ref.1, bf16[2,512,128]{2,1,0:T(8,128)(2,1)} %constant.18.clone.core_any, ...), custom_call_target="tpu_custom_call" | custom-call | tf_op jit(solution)/shard_map/pallas_call | solution.py:381
  40.4 1.7 %copy.16 = f32[512,128]{1,0:T(8,128)} copy(f32[512,128]{1,0:T(8,128)} %shard_map.136) | data formatting | bytes 524288
